TPU v7x, 32 devices: a whole 2x2x4 slice. The times are simulated.
32 devices in a mesh: rows: 8 (over z, y), grp: 4 (over x, core).
Axes of the slice: x: 2, y: 2, z: 4, core: 2. Of those that a mesh axis runs over, the one named last changes fastest.
Arguments:
- features: bfloat16 [4096, 512], P(('rows', 'grp')), may hold values from -6 to 6
- tile_entries: bfloat16 [64, 64, 1024], P(('rows', 'grp'))
- tile_columns: int32 [64, 16], P(('rows', 'grp')), may hold values from 0 to 63, as said below
- tiles_per_row: int32 [64], P(('rows', 'grp')), may hold values from 1 to 16, as said below
- rev_vals: bfloat16 [64, 64, 1024], P(('rows', 'grp'))
- rev_cols: int32 [64, 16], P(('rows', 'grp')), may hold values from 0 to 63, as said below
- rev_count: int32 [64], P(('rows', 'grp')), may hold values from 1 to 16, as said below
- w_first: bfloat16 [512, 512], replicated, may hold values from -0.25 to 0.25
- w_second: bfloat16 [512, 512], replicated, may hold values from -0.25 to 0.25
- cotangent: bfloat16 [4096, 512], P(('rows', 'grp')), may hold values from -0.09375 to 0.09375
Outputs:
- z_out: bfloat16 [4096, 512], P(('rows', 'grp'))
- grad_first: float32 [512, 512], replicated
- grad_second: float32 [512, 512], replicated
Inputs may be any that keep to these rules, and one draw needn't show every extreme that they name: `tile_columns`: within each block row the 16 slots name distinct block columns; for each slot s, the block columns named in slot s over all block rows are all different. `tiles_per_row`: some block row has exactly 16 tiles. `rev_cols`: within each block column the slots name distinct block rows; the live transposed slots of block column c hold exactly the transposes of the live tiles of A in block column c. `rev_count`: some block column has exactly 16 tiles.
All inputs are finite; a program needn't handle non-finite values.
Results may differ from a plain program's by a relative error of at most 0.0062.
Values may be sent and summed in bfloat16 or wider, within the bound.
No kernel may reach another device: no remote copies, remote signals or barrier semaphores. Data moves between devices by JAX's collectives and lax.ppermute only.
A program may use at most 128 MiB of HBM per device.

v0:
```python
import jax
import jax.numpy as jnp
from jax import lax
from jax.sharding import PartitionSpec as P


def active_mask(columns, counts):
    return lax.broadcasted_iota(jnp.int32, columns.shape, 1) < counts[:, None]


def aggregate(panel_vals, strip_columns, strip_count, everyone, own_rows):
    blocks, size_block, span_width = panel_vals.shape
    slot_count = span_width // size_block
    channels = everyone.shape[1]
    block_table = everyone.reshape(-1, size_block, channels)
    weights = active_mask(strip_columns, strip_count).astype(everyone.dtype)
    picked = (block_table[strip_columns] * weights[:, :, None, None]).reshape(
        blocks, slot_count * size_block, channels
    )
    summed_rows = jnp.einsum("bik,bkc->bic", panel_vals, picked, preferred_element_type=jnp.float32)
    return summed_rows.reshape(blocks * size_block, channels) + own_rows.astype(jnp.float32)


def spread_terms(panel_vals, strip_columns, strip_count, grad_rows):
    blocks, size_block, span_width = panel_vals.shape
    slot_count = span_width // size_block
    channels = grad_rows.shape[1]
    products = jnp.einsum(
        "bik,bic->bkc",
        panel_vals,
        grad_rows.reshape(blocks, size_block, channels),
        preferred_element_type=jnp.float32,
    )
    products = products.reshape(blocks * slot_count, size_block, channels)
    targets = strip_columns.reshape(-1)
    slot_active = active_mask(strip_columns, strip_count).reshape(-1)

    def term_rows(first_row, row_count):
        segment_ids = row_count // size_block
        slot_offset = targets - first_row // size_block
        inside_bound = slot_active & (slot_offset >= 0) & (slot_offset < segment_ids)
        labels = jnp.where(inside_bound, slot_offset, segment_ids)
        summed_rows = jax.ops.segment_sum(products, labels, num_segments=segment_ids + 1)
        return summed_rows[:segment_ids].reshape(row_count, channels)

    return term_rows


def silu_slope(values):
    sigmoid_part = jax.nn.sigmoid(values)
    return sigmoid_part * (1.0 + values * (1.0 - sigmoid_part))


def to_columns(row_block):
    return lax.all_to_all(row_block, "grp", split_axis=1, concat_axis=0, tiled=True)


def mix_columns(column_block, panel_vals, strip_columns, strip_count):
    everyone = lax.all_gather(column_block, "rows", axis=0, tiled=True)
    return aggregate(panel_vals, strip_columns, strip_count, everyone, column_block)


def shards(
    features,
    tile_entries,
    tile_columns,
    tiles_per_row,
    rev_vals,
    rev_cols,
    rev_count,
    w_first,
    w_second,
    cotangent,
):
    panel_vals, strip_columns, strip_count = (
        lax.all_gather(tile_entries, "grp", axis=0, tiled=True),
        lax.all_gather(tile_columns, "grp", axis=0, tiled=True),
        lax.all_gather(tiles_per_row, "grp", axis=0, tiled=True),
    )

    def propagate(row_block):
        column_block = to_columns(row_block)
        summed_rows = mix_columns(column_block, panel_vals, strip_columns, strip_count).astype(
            jnp.bfloat16
        )
        return lax.all_to_all(summed_rows, "grp", split_axis=0, concat_axis=1, tiled=True)

    mixed_first = propagate(features)
    pre_first = jnp.dot(mixed_first, w_first, preferred_element_type=jnp.float32)
    hidden = jax.nn.silu(pre_first).astype(jnp.bfloat16)
    mixed_second = propagate(hidden)
    z_out = jnp.dot(mixed_second, w_second, preferred_element_type=jnp.float32).astype(jnp.bfloat16)
    local_second = jnp.einsum(
        "nh,nk->hk", mixed_second, cotangent, preferred_element_type=jnp.float32
    )
    grad_second = lax.psum(local_second, ("rows", "grp"))
    back_second = jnp.dot(cotangent, w_second.T, preferred_element_type=jnp.float32).astype(
        jnp.bfloat16
    )
    column_block = to_columns(back_second)
    term_rows = spread_terms(panel_vals, strip_columns, strip_count, column_block)
    summed_rows = lax.psum_scatter(
        term_rows(jnp.int32(0), column_block.shape[0] * lax.axis_size("rows")),
        "rows",
        scatter_dimension=0,
        tiled=True,
    )
    summed_rows = summed_rows + column_block.astype(jnp.float32)
    back_hidden = lax.all_to_all(summed_rows, "grp", split_axis=0, concat_axis=1, tiled=True)
    back_first = (back_hidden * silu_slope(pre_first)).astype(jnp.bfloat16)
    local_first = jnp.einsum(
        "nh,nk->hk", mixed_first, back_first, preferred_element_type=jnp.float32
    )
    grad_first = lax.psum(local_first, ("rows", "grp"))
    return (z_out, grad_first, grad_second)


def solution(mesh):
    placed = (
        P(("rows", "grp"), None),
        P(("rows", "grp"), None, None),
        P(("rows", "grp"), None),
        P(("rows", "grp")),
        P(("rows", "grp"), None, None),
        P(("rows", "grp"), None),
        P(("rows", "grp")),
        P(),
        P(),
        P(("rows", "grp"), None),
    )
    return jax.shard_map(
        shards,
        mesh=mesh,
        in_specs=placed,
        out_specs=(P(("rows", "grp"), None), P(), P()),
        check_vma=False,
    )
```

profile of v0, /device:TPU:0, one launch (start us, length us, event | category | flops | bytes accessed | tf_op | source)
XLA Modules:
  0.0 358.8 jit_solution(1867615093499603882)
XLA Ops:
  7.2 1.1 copy.33
  8.3 8.6 %all_to_all.105 = bf16[128,4,128]{0,2,1:T(8,128)(2,1)S(1)} all-to-all(bf16[128,4,128]{0,2,1:T(8,128)(2,1)S(1)} %bitcast.96), channel_id=1, replica_groups=mesh['rows'=8,'grp'=4] {'grp'}, dimensions={1} | all-to-all | bytes 262144 | tf_op jit(solution)/shard_map/all_to_all | solution.py:55
  16.9 0.8 copy.34
  17.8 0.7 all-gather.7.cloned.1.call-update
  18.5 1.2 dynamic-slice
  20.4 0.9 dynamic-update-slice
  21.3 4.3 %all-reduce = s32[8]{0:T(128)S(1)} all-reduce(s32[8]{0:T(128)S(1)} %dynamic-update-slice), channel_id=1, replica_groups=mesh['rows'=8,'grp'=4] {'grp'}, use_global_device_ids=true, to_apply=%add | all-reduce | flops 8 | bytes 64
  25.6 5.3 %all-gather = s32[4,2,16]{2,1,0:T(2,128)S(1)} all-gather(s32[1,2,16]{2,1,0:T(2,128)} %bitcast.98), channel_id=1, replica_groups=mesh['rows'=8,'grp'=4] {'grp'}, dimensions={0}, use_global_device_ids=true | all-gather | bytes 640 | tf_op jit(solution)/shard_map/all_gather | solution.py:77
  30.8 0.1 reshape.145
  31.0 0.1 mul.33
  31.1 0.1 mul.34
  31.2 27.2 %all-gather.5.cloned.1.call-done = bf16[4096,128]{1,0:T(8,128)(2,1)} async-done(((bf16[512,128]{1,0:T(8,128)(2,1)}), bf16[4096,128]{1,0:T(8,128)(2,1)}) %all-gather.5.cloned.1.call-update) | async-done | bytes 1048592 | tf_op jit(solution)/shard_map/all_gather | solution.py:59
  58.4 2.2 gather_fusion
  60.6 2.2 bitcast_multiply_fusion.1
  62.8 12.7 %all-gather.7.cloned.1.call-done = bf16[8,64,1024]{2,1,0:T(8,128)(2,1)} async-done(((bf16[2,64,1024]{2,1,0:T(8,128)(2,1)}), bf16[8,64,1024]{2,1,0:T(8,128)(2,1)}) %all-gather.7.cloned.1.call-update) | async-done | bytes 1048592 | tf_op jit(solution)/shard_map/all_gather | solution.py:76
  75.5 2.4 fusion.11
  77.9 0.1 copy.35
  78.1 7.2 %all_to_all.106 = bf16[4,128,128]{1,2,0:T(8,128)(2,1)S(1)} all-to-all(bf16[4,128,128]{1,2,0:T(8,128)(2,1)S(1)} %add_convert_fusion.1), channel_id=1, replica_groups=mesh['rows'=8,'grp'=4] {'grp'}, dimensions={0} | all-to-all | bytes 262144 | tf_op jit(solution)/shard_map/all_to_all | solution.py:86
  85.3 0.2 fusion.9
  85.6 7.7 %all_to_all.107 = bf16[128,4,128]{2,0,1:T(8,128)(2,1)} all-to-all(bf16[128,4,128]{2,0,1:T(8,128)(2,1)S(1)} %copy_bitcast_fusion.1), channel_id=1, replica_groups=mesh['rows'=8,'grp'=4] {'grp'}, dimensions={1} | all-to-all | bytes 262144 | tf_op jit(solution)/shard_map/all_to_all | solution.py:55
  93.3 0.3 fusion
  93.6 0.7 copy.48
  94.3 3.3 all-to-all-start.4
  97.7 0.1 reshape.138
  97.8 0.1 lt.51
  97.9 4.4 %all-to-all-done.4 = bf16[128,4,128]{2,0,1:T(8,128)(2,1)S(1)} async-done(((bf16[128,4,128]{2,0,1:T(8,128)(2,1)}), bf16[128,4,128]{2,0,1:T(8,128)(2,1)S(1)}, u32[]{:S(2)}, u32[]{:S(2)}) %all-to-all-start.4) | async-done | bytes 131104 | tf_op jit(solution)/shard_map/all_to_all | solution.py:55
  102.3 2.7 convolution_bitcast_fusion
  105.0 5.4 %copy.39 = f32[8,1024,128]{2,1,0:T(8,128)} copy(f32[8,1024,128]{1,2,0:T(8,128)} %convolution_bitcast_fusion) | data formatting | bytes 8388608 | tf_op jit(solution)/shard_map/bik,bic->bkc/dot_general | solution.py:28
  110.3 0.2 broadcast_in_dim.6
  110.6 13.6 %scatter_fusion = f32[65,64,128]{2,1,0:T(8,128)S(1)} fusion(f32[65,64,128]{2,1,0:T(8,128)S(1)} %broadcast_in_dim.6, s32[128]{0:T(128)S(1)} %fusion.6, f32[128,64,128]{2,1,0:T(8,128)} %bitcast.79), kind=kCustom, calls=%fused_computation.2 | custom fusion | flops 1048576 | bytes 12583424 | tf_op jit(solution)/shard_map/scatter-add | solution.py:43
  124.2 1.5 slice.8
  125.7 7.9 %all-gather.9.cloned.1.call-done = bf16[4096,128]{1,0:T(8,128)(2,1)} async-done(((bf16[512,128]{1,0:T(8,128)(2,1)}), bf16[4096,128]{1,0:T(8,128)(2,1)}) %all-gather.9.cloned.1.call-update) | async-done | bytes 1048592 | tf_op jit(solution)/shard_map/all_gather | solution.py:59
  133.6 2.2 gather_fusion.1
  135.8 1.6 bitcast_multiply_fusion
  137.5 0.5 fusion.12
  138.0 0.4 copy-done.3
  138.4 7.2 %all_to_all.108 = bf16[4,128,128]{2,1,0:T(8,128)(2,1)S(1)} all-to-all(bf16[4,128,128]{2,1,0:T(8,128)(2,1)S(1)} %add_convert_fusion), channel_id=1, replica_groups=mesh['rows'=8,'grp'=4] {'grp'}, dimensions={0} | all-to-all | bytes 262144 | tf_op jit(solution)/shard_map/all_to_all | solution.py:86
  145.5 0.1 copy.37
  145.7 58.0 %reduce-scatter.2.cloned.1.call-done = f32[512,128]{1,0:T(8,128)} async-done(((f32[4096,128]{1,0:T(8,128)}), f32[512,128]{1,0:T(8,128)}) %reduce-scatter.2.cloned.1.call-update) | async-done | bytes 262160 | tf_op jit(solution)/shard_map/reduce_scatter | solution.py:102
  203.7 1.7 convert_add_fusion
  205.4 3.4 all-to-all-start.5
  208.8 1.3 fusion.10
  210.1 4.7 %all-to-all-done.5 = f32[4,128,128]{2,1,0:T(8,128)S(1)} async-done(((f32[4,128,128]{2,1,0:T(8,128)}), f32[4,128,128]{2,1,0:T(8,128)S(1)}, u32[]{:S(2)}, u32[]{:S(2)}) %all-to-all-start.5) | async-done | bytes 262176 | tf_op jit(solution)/shard_map/all_to_all | solution.py:109
  214.8 1.3 fusion.2
  216.1 0.9 convolution_convert_fusion.1
  217.0 131.9 %all-reduce.4.cloned.1.call-done = (f32[512,512]{1,0:T(8,128)}, f32[512,512]{1,0:T(8,128)}) async-done(((f32[512,512]{1,0:T(8,128)}, f32[512,512]{1,0:T(8,128)}), (f32[512,512]{1,0:T(8,128)}, f32[512,512]{1,0:T(8,128)})) %all-reduce.4.cloned.1.call-update) | async-done | bytes 2097168 | tf_op jit(solution)/shard_map/psum | solution.py:114
  348.9 2.4 copy.53
  351.3 1.0 copy.54
  (30 shorter events, 0.5 us)
Async XLA Ops:
  7.2 86.1 %copy-start = (bf16[512,512]{1,0:T(8,128)(2,1)S(1)}, bf16[512,512]{1,0:T(8,128)(2,1)}, u32[]{:S(2)}) copy-start(bf16[512,512]{1,0:T(8,128)(2,1)} %param.15) | copy-start | bytes 1572868
  7.2 51.3 %all-gather.5.cloned.1.call-start = ((), (), s32[]{:S(2)}) async-start(), calls=%async_computation.7 | async-start | bytes 1179648 | tf_op jit(solution)/shard_map/all_gather | solution.py:59
  17.7 57.8 %all-gather.7.cloned.1.call-start = ((), (), s32[]{:S(2)}) async-start(), calls=%async_computation.8 | async-start | bytes 1310720 | tf_op jit(solution)/shard_map/all_gather | solution.py:76
  18.5 115.1 %all-gather.9.cloned.1.call-start = ((), (), s32[]{:S(2)}) async-start(), calls=%async_computation.9 | async-start | bytes 1179648 | tf_op jit(solution)/shard_map/all_gather | solution.py:59
  62.8 22.4 %copy-start.5 = (bf16[512,512]{1,0:T(8,128)(2,1)S(1)}, bf16[512,512]{1,0:T(8,128)(2,1)}, u32[]{:S(2)}) copy-start(bf16[512,512]{1,0:T(8,128)(2,1)} %param.14) | copy-start | bytes 1572868
  77.9 15.4 %copy-start.6 = (bf16[128,512]{1,0:T(8,128)(2,1)S(1)}, bf16[128,512]{1,0:T(8,128)(2,1)}, u32[]{:S(2)}) copy-start(bf16[128,512]{1,0:T(8,128)(2,1)} %param.16) | copy-start | bytes 393220
  77.9 24.3 %copy-start.1 = (bf16[8,64,1024]{2,1,0:T(8,128)(2,1)S(1)}, bf16[8,64,1024]{2,1,0:T(8,128)(2,1)}, u32[]{:S(2)}) copy-start(bf16[8,64,1024]{2,1,0:T(8,128)(2,1)} %all-gather.7.cloned.1.call-done) | copy-start | bytes 3145732
  94.3 7.9 %all-to-all-start.4 = ((bf16[128,4,128]{2,0,1:T(8,128)(2,1)}), bf16[128,4,128]{2,0,1:T(8,128)(2,1)S(1)}, u32[]{:S(2)}, u32[]{:S(2)}) async-start(bf16[128,4,128]{2,0,1:T(8,128)(2,1)} %bitcast.76), calls=%async_computation.4 | async-start | bytes 262144 | tf_op jit(solution)/shard_map/all_to_all | solution.py:55
  97.7 106.0 %reduce-scatter.2.cloned.1.call-start = ((), (), s32[]{:S(2)}) async-start(), calls=%async_computation.10 | async-start | bytes 2359296 | tf_op jit(solution)/shard_map/reduce_scatter | solution.py:102
  135.8 1.6 copy-start.2
  137.4 0.9 copy-start.3
  205.4 9.4 %all-to-all-start.5 = ((f32[4,128,128]{2,1,0:T(8,128)}), f32[4,128,128]{2,1,0:T(8,128)S(1)}, u32[]{:S(2)}, u32[]{:S(2)}) async-start(f32[4,128,128]{2,1,0:T(8,128)} %bitcast.28), calls=%async_computation.6 | async-start | bytes 524288 | tf_op jit(solution)/shard_map/all_to_all | solution.py:109
  208.8 140.1 %all-reduce.4.cloned.1.call-start = ((), (), s32[]{:S(2)}) async-start(), calls=%async_computation.11 | async-start | bytes 4194304 | tf_op jit(solution)/shard_map/psum | solution.py:114
  348.9 2.4 copy-start.4
Sparse Core Ops, SparseCore 0:
  17.9 40.5 all-gather.4
  60.0 15.4 all-gather.6
  93.4 40.1 all-gather.8
  137.0 66.6 reduce-scatter.1
  216.3 132.6 all-reduce.3
where the time goes:
time: 360 us; the launch traced here: 359 us
  waiting for transfers between devices  247 us (69%)
  blocking collectives  40.2 us (11%)
  local copies, waits for them, and re-layouts  20.5 us (6%)
  other arithmetic  19.3 us (5%)
  between operations  14.7 us (4%)
  matrix products  9.67 us (3%)
  starting transfers between devices  6.93 us (2%)
    psum x1, waiting for transfers between devices, shards(): grad_first = lax.psum(local_first, ('rows', 'grp'))  132 us
    reduce_scatter x1, waiting for transfers between devices, shards(): lax.psum_scatter(term_rows(jnp.int32(0), column_block.shape[0] * lax.axis...  58 us
    all_gather x2, waiting for transfers between devices, mix_columns(): everyone = lax.all_gather(column_block, 'rows', axis=0, tiled=True)  35.2 us
    all_to_all x2, blocking collectives, to_columns(): lax.all_to_all(row_block, 'grp', split_axis=1, concat_axis=0, tiled=True)  16.3 us
    all_to_all x2, blocking collectives, propagate(): lax.all_to_all(summed_rows, 'grp', split_axis=0, concat_axis=1, tiled=True)  14.3 us
    scatter-add x1, other arithmetic, term_rows(): jax.ops.segment_sum(products, labels, num_segments=segment_ids + 1)  13.6 us
    all_gather x1, waiting for transfers between devices, shards(): lax.all_gather(tile_entries, 'grp', axis=0, tiled=True)  12.7 us
  transfers between devices with their start and end apart: 7, of which 7 were waited for; matrix products, arithmetic and copies ran while one was open for 11% of the time, Pallas kernels for 0%

commit v1 on v0

--- a/solution.py
+++ b/solution.py
@@ -111,7 +111,7 @@
     local_first = jnp.einsum(
         "nh,nk->hk", mixed_first, back_first, preferred_element_type=jnp.float32
     )
-    grad_first = lax.psum(local_first, ("rows", "grp"))
+    grad_first = lax.psum(lax.psum(local_first, "grp"), "rows")
     return (z_out, grad_first, grad_second)
 
 

time: 360 us -> 479 us (1.33)
  waiting for transfers between devices: 247 us -> 360 us
    psum x1 -> x3, waiting for transfers between devices: 132 us -> 241 us  [the longest x1 136 us: shards(): grad_second = lax.psum(local_second, ('rows', 'grp'))]
    reduce_scatter x1, waiting for transfers between devices: 58 us -> 63 us  [shards(): lax.psum_scatter(term_rows(jnp.int32(0), column_block.shape[0] * lax.axis...]
  transfers between devices with their start and end apart: 7 -> 9, of which waited for: 7 -> 9; matrix products, arithmetic and copies ran while one was open for 11% -> 9% of each run, Pallas kernels for 0% -> 0%
where the time goes in v1:
time: 479 us; the launch traced here: 478 us
  waiting for transfers between devices  360 us (75%)
  blocking collectives  41.4 us (9%)
  other arithmetic  21.3 us (4%)
  local copies, waits for them, and re-layouts  21.2 us (4%)
  between operations  15 us (3%)
  matrix products  11.3 us (2%)
  starting transfers between devices  7.02 us (1%)
    psum x1, waiting for transfers between devices, shards(): grad_second = lax.psum(local_second, ('rows', 'grp'))  136 us
    psum x2, waiting for transfers between devices, shards(): grad_first = lax.psum(lax.psum(local_first, 'grp'), 'rows')  105 us
    reduce_scatter x1, waiting for transfers between devices, shards(): lax.psum_scatter(term_rows(jnp.int32(0), column_block.shape[0] * lax.axis...  63 us
    all_gather x2, waiting for transfers between devices, mix_columns(): everyone = lax.all_gather(column_block, 'rows', axis=0, tiled=True)  35.2 us
    all_to_all x2, blocking collectives, to_columns(): lax.all_to_all(row_block, 'grp', split_axis=1, concat_axis=0, tiled=True)  16.3 us
    all_to_all x2, blocking collectives, propagate(): lax.all_to_all(summed_rows, 'grp', split_axis=0, concat_axis=1, tiled=True)  15.5 us
    scatter-add x1, other arithmetic, term_rows(): jax.ops.segment_sum(products, labels, num_segments=segment_ids + 1)  13.6 us
    all_gather x1, waiting for transfers between devices, shards(): lax.all_gather(tile_entries, 'grp', axis=0, tiled=True)  12.6 us
  transfers between devices with their start and end apart: 9, of which 9 were waited for; matrix products, arithmetic and copies ran while one was open for 9% of the time, Pallas kernels for 0%

profile of v1, /device:TPU:0, one launch (start us, length us, event | category | flops | bytes accessed | tf_op | source)
XLA Modules:
  0.0 477.5 jit_solution(8750863073374898143)
XLA Ops:
  7.2 1.1 copy.33
  8.3 8.6 %all_to_all.105 = bf16[128,4,128]{0,2,1:T(8,128)(2,1)S(1)} all-to-all(bf16[128,4,128]{0,2,1:T(8,128)(2,1)S(1)} %bitcast.96), channel_id=1, replica_groups=mesh['rows'=8,'grp'=4] {'grp'}, dimensions={1} | all-to-all | bytes 262144 | tf_op jit(solution)/shard_map/all_to_all | solution.py:55
  16.9 0.8 copy.34
  17.8 0.7 all-gather.7.cloned.1.call-update
  18.5 1.2 dynamic-slice
  20.4 0.9 dynamic-update-slice
  21.3 4.3 all-reduce
  25.6 5.3 %all-gather = s32[4,2,16]{2,1,0:T(2,128)S(1)} all-gather(s32[1,2,16]{2,1,0:T(2,128)} %bitcast.98), channel_id=1, replica_groups=mesh['rows'=8,'grp'=4] {'grp'}, dimensions={0}, use_global_device_ids=true | all-gather | bytes 640 | tf_op jit(solution)/shard_map/all_gather | solution.py:77
  31.0 0.1 mul.33
  31.1 0.1 mul.34
  31.2 27.2 %all-gather.5.cloned.1.call-done = bf16[4096,128]{1,0:T(8,128)(2,1)} async-done(((bf16[512,128]{1,0:T(8,128)(2,1)}), bf16[4096,128]{1,0:T(8,128)(2,1)}) %all-gather.5.cloned.1.call-update) | async-done | bytes 1048592 | tf_op jit(solution)/shard_map/all_gather | solution.py:59
  58.4 2.2 gather_fusion
  60.6 2.3 bitcast_multiply_fusion.1
  62.9 12.6 %all-gather.7.cloned.1.call-done = bf16[8,64,1024]{2,1,0:T(8,128)(2,1)} async-done(((bf16[2,64,1024]{2,1,0:T(8,128)(2,1)}), bf16[8,64,1024]{2,1,0:T(8,128)(2,1)}) %all-gather.7.cloned.1.call-update) | async-done | bytes 1048592 | tf_op jit(solution)/shard_map/all_gather | solution.py:76
  75.5 2.4 fusion.11
  77.9 0.1 copy.35
  78.1 7.2 %all_to_all.106 = bf16[4,128,128]{1,2,0:T(8,128)(2,1)S(1)} all-to-all(bf16[4,128,128]{1,2,0:T(8,128)(2,1)S(1)} %add_convert_fusion.1), channel_id=1, replica_groups=mesh['rows'=8,'grp'=4] {'grp'}, dimensions={0} | all-to-all | bytes 262144 | tf_op jit(solution)/shard_map/all_to_all | solution.py:86
  85.3 0.2 fusion.9
  85.6 7.7 %all_to_all.107 = bf16[128,4,128]{2,0,1:T(8,128)(2,1)} all-to-all(bf16[128,4,128]{2,0,1:T(8,128)(2,1)S(1)} %copy_bitcast_fusion.1), channel_id=1, replica_groups=mesh['rows'=8,'grp'=4] {'grp'}, dimensions={1} | all-to-all | bytes 262144 | tf_op jit(solution)/shard_map/all_to_all | solution.py:55
  93.3 0.3 fusion
  93.6 0.7 copy.48
  94.3 3.3 all-to-all-start.4
  97.7 0.1 reshape.138
  97.8 0.1 lt.51
  97.9 4.4 all-to-all-done.4
  102.2 2.7 convolution_bitcast_fusion
  105.0 5.4 %copy.39 = f32[8,1024,128]{2,1,0:T(8,128)} copy(f32[8,1024,128]{1,2,0:T(8,128)} %convolution_bitcast_fusion) | data formatting | bytes 8388608 | tf_op jit(solution)/shard_map/bik,bic->bkc/dot_general | solution.py:28
  110.3 0.2 broadcast_in_dim.6
  110.6 13.6 %scatter_fusion = f32[65,64,128]{2,1,0:T(8,128)S(1)} fusion(f32[65,64,128]{2,1,0:T(8,128)S(1)} %broadcast_in_dim.6, s32[128]{0:T(128)S(1)} %fusion.6, f32[128,64,128]{2,1,0:T(8,128)} %bitcast.79), kind=kCustom, calls=%fused_computation.2 | custom fusion | flops 1048576 | bytes 12583424 | tf_op jit(solution)/shard_map/scatter-add | solution.py:43
  124.2 1.5 slice.8
  125.7 8.0 %all-gather.9.cloned.1.call-done = bf16[4096,128]{1,0:T(8,128)(2,1)} async-done(((bf16[512,128]{1,0:T(8,128)(2,1)}), bf16[4096,128]{1,0:T(8,128)(2,1)}) %all-gather.9.cloned.1.call-update) | async-done | bytes 1048592 | tf_op jit(solution)/shard_map/all_gather | solution.py:59
  133.6 3.4 gather_fusion.1
  137.0 3.5 bitcast_multiply_fusion
  140.5 63.0 %reduce-scatter.2.cloned.1.call-done = f32[512,128]{1,0:T(8,128)} async-done(((f32[4096,128]{1,0:T(8,128)}), f32[512,128]{1,0:T(8,128)}) %reduce-scatter.2.cloned.1.call-update) | async-done | bytes 262160 | tf_op jit(solution)/shard_map/reduce_scatter | solution.py:102
  203.5 1.7 convert_add_fusion
  205.2 3.4 all-to-all-start.5
  208.7 2.1 fusion.12
  210.8 3.8 all-to-all-done.5
  214.6 1.3 fusion.2
  216.1 8.4 %all_to_all.108 = bf16[4,128,128]{2,1,0:T(8,128)(2,1)S(1)} all-to-all(bf16[4,128,128]{2,1,0:T(8,128)(2,1)S(1)} %add_convert_fusion), channel_id=1, replica_groups=mesh['rows'=8,'grp'=4] {'grp'}, dimensions={0} | all-to-all | bytes 262144 | tf_op jit(solution)/shard_map/all_to_all | solution.py:86
  224.4 0.1 copy.37
  224.6 1.3 fusion.10
  225.9 24.4 %all-reduce.5.cloned.1.call-done = f32[512,512]{1,0:T(8,128)} async-done(((f32[512,512]{1,0:T(8,128)}), f32[512,512]{1,0:T(8,128)}) %all-reduce.5.cloned.1.call-update) | async-done | bytes 1048592 | tf_op jit(solution)/shard_map/psum | solution.py:114
  250.3 0.9 convolution_convert_fusion.1
  251.2 135.7 %all-reduce.9.cloned.1.call-done = f32[512,512]{1,0:T(8,128)} async-done(((f32[512,512]{1,0:T(8,128)}), f32[512,512]{1,0:T(8,128)}) %all-reduce.9.cloned.1.call-update) | async-done | bytes 1048592 | tf_op jit(solution)/shard_map/psum | solution.py:96
  386.9 80.5 %all-reduce.7.cloned.1.call-done = f32[512,512]{1,0:T(8,128)} async-done(((f32[512,512]{1,0:T(8,128)}), f32[512,512]{1,0:T(8,128)}) %all-reduce.7.cloned.1.call-update) | async-done | bytes 1048592 | tf_op jit(solution)/shard_map/psum | solution.py:114
  467.5 2.3 copy.54
  469.7 1.0 copy.55
  (36 shorter events, 0.7 us)
Async XLA Ops:
  7.2 86.1 %copy-start = (bf16[512,512]{1,0:T(8,128)(2,1)S(1)}, bf16[512,512]{1,0:T(8,128)(2,1)}, u32[]{:S(2)}) copy-start(bf16[512,512]{1,0:T(8,128)(2,1)} %param.15) | copy-start | bytes 1572868
  7.2 51.3 %all-gather.5.cloned.1.call-start = ((), (), s32[]{:S(2)}) async-start(), calls=%async_computation.7 | async-start | bytes 1179648 | tf_op jit(solution)/shard_map/all_gather | solution.py:59
  17.7 57.8 %all-gather.7.cloned.1.call-start = ((), (), s32[]{:S(2)}) async-start(), calls=%async_computation.8 | async-start | bytes 1310720 | tf_op jit(solution)/shard_map/all_gather | solution.py:76
  18.5 115.1 %all-gather.9.cloned.1.call-start = ((), (), s32[]{:S(2)}) async-start(), calls=%async_computation.9 | async-start | bytes 1179648 | tf_op jit(solution)/shard_map/all_gather | solution.py:59
  62.9 22.4 %copy-start.5 = (bf16[512,512]{1,0:T(8,128)(2,1)S(1)}, bf16[512,512]{1,0:T(8,128)(2,1)}, u32[]{:S(2)}) copy-start(bf16[512,512]{1,0:T(8,128)(2,1)} %param.14) | copy-start | bytes 1572868
  77.9 15.4 %copy-start.6 = (bf16[128,512]{1,0:T(8,128)(2,1)S(1)}, bf16[128,512]{1,0:T(8,128)(2,1)}, u32[]{:S(2)}) copy-start(bf16[128,512]{1,0:T(8,128)(2,1)} %param.16) | copy-start | bytes 393220
  77.9 24.3 %copy-start.1 = (bf16[8,64,1024]{2,1,0:T(8,128)(2,1)S(1)}, bf16[8,64,1024]{2,1,0:T(8,128)(2,1)}, u32[]{:S(2)}) copy-start(bf16[8,64,1024]{2,1,0:T(8,128)(2,1)} %all-gather.7.cloned.1.call-done) | copy-start | bytes 3145732
  94.3 7.9 %all-to-all-start.4 = ((bf16[128,4,128]{2,0,1:T(8,128)(2,1)}), bf16[128,4,128]{2,0,1:T(8,128)(2,1)S(1)}, u32[]{:S(2)}, u32[]{:S(2)}) async-start(bf16[128,4,128]{2,0,1:T(8,128)(2,1)} %bitcast.76), calls=%async_computation.4 | async-start | bytes 262144 | tf_op jit(solution)/shard_map/all_to_all | solution.py:55
  97.6 105.9 %reduce-scatter.2.cloned.1.call-start = ((), (), s32[]{:S(2)}) async-start(), calls=%async_computation.10 | async-start | bytes 2359296 | tf_op jit(solution)/shard_map/reduce_scatter | solution.py:102
  137.0 71.7 %copy-start.2 = (bf16[8,64,1024]{2,1,0:T(8,128)(2,1)S(1)}, bf16[8,64,1024]{2,1,0:T(8,128)(2,1)}, u32[]{:S(2)}) copy-start(bf16[8,64,1024]{2,1,0:T(8,128)(2,1)} %all-gather.7.cloned.1.call-done) | copy-start | bytes 3145732
  205.2 9.4 %all-to-all-start.5 = ((f32[4,128,128]{2,1,0:T(8,128)}), f32[4,128,128]{2,1,0:T(8,128)S(1)}, u32[]{:S(2)}, u32[]{:S(2)}) async-start(f32[4,128,128]{2,1,0:T(8,128)} %bitcast.28), calls=%async_computation.6 | async-start | bytes 524288 | tf_op jit(solution)/shard_map/all_to_all | solution.py:109
  208.6 41.7 %all-reduce.5.cloned.1.call-start = ((), (), s32[]{:S(2)}) async-start(), calls=%async_computation.11 | async-start | bytes 2097152 | tf_op jit(solution)/shard_map/psum | solution.py:114
  210.8 5.3 %copy-start.3 = (bf16[128,4,128]{2,0,1:T(8,128)(2,1)S(1)}, bf16[128,4,128]{2,0,1:T(8,128)(2,1)}, u32[]{:S(2)}) copy-start(bf16[128,4,128]{2,0,1:T(8,128)(2,1)} %all_to_all.107) | copy-start | bytes 393220
  216.0 171.0 %all-reduce.9.cloned.1.call-start = ((), (), s32[]{:S(2)}) async-start(), calls=%async_computation.13 | async-start | bytes 2097152 | tf_op jit(solution)/shard_map/psum | solution.py:96
  225.9 241.6 %all-reduce.7.cloned.1.call-start = ((), (), s32[]{:S(2)}) async-start(), calls=%async_computation.12 | async-start | bytes 2097152 | tf_op jit(solution)/shard_map/psum | solution.py:114
  386.9 82.8 %copy-start.4 = (f32[512,512]{1,0:T(8,128)S(1)}, f32[512,512]{1,0:T(8,128)}, u32[]{:S(2)}) copy-start(f32[512,512]{1,0:T(8,128)} %all-reduce.9.cloned.1.call-done) | copy-start | bytes 3145732
Sparse Core Ops, SparseCore 0:
  17.9 40.5 all-gather.4
  60.0 15.4 all-gather.6
  93.4 40.1 all-gather.8
  137.0 66.4 reduce-scatter.1
  216.1 34.1 all-reduce.4
  256.7 130.1 all-reduce.8
  390.4 76.9 all-reduce.6
